TPU v7x, 32 devices: a whole 2x2x4 slice. The times are simulated.
32 devices in a mesh: ia: 4 (over y, core), ja: 2 (over x), ka: 4 (over z).
Axes of the slice: x: 2, y: 2, z: 4, core: 2. Of those that a mesh axis runs over, the one named last changes fastest.
Arguments:
- block_coords: int32 [4, 2, 4, 4, 3], P('ia', 'ja', 'ka'), may hold values from 0 to 3, as said below
- live_blocks: int32 [4, 2, 4], P('ia', 'ja', 'ka'), may hold values from 1 to 4, as said below
- counts: int32 [4, 2, 4, 4, 64, 4096], P('ia', 'ja', 'ka'), may hold values from 0 to 7
- factor_a: float32 [1024, 256], P(('ia', 'ja', 'ka')), may hold values from 0.3 to 9.6
- factor_b: float32 [512, 256], P(('ja', 'ka')), may hold values from 0.05 to 8
- factor_c: float32 [1024, 256], P('ka', 'ia'), may hold values from 0.05 to 8
Outputs:
- factor_new: float32 [1024, 256], P(('ia', 'ja', 'ka'))
Inputs may be any that keep to these rules, and one draw needn't show every extreme that they name: `block_coords`: a device's slots name distinct blocks; slot 0 is always live, and every mode-1 block of the slab has a live block on some device. `live_blocks`: on some device all 4 slots are live.
All inputs are finite; a program needn't handle non-finite values.
Results may differ from a plain program's by a relative error of at most 0.00061.
Values may be sent and summed in bfloat16 or wider, within the bound.
A program may use at most 64 MiB of HBM per device.

v0:
```python
import jax
import jax.numpy as jnp
from jax import lax
from jax.sharding import PartitionSpec as P

R = 256
BS = 64
RB1 = 4
RB2 = 4
RB3 = 4
SLOTS = 4


def make_panel(rows_b, rows_c, index_j, index_k):
    piece_b = lax.dynamic_slice_in_dim(rows_b, index_j * BS, BS, 0)
    piece_c = lax.dynamic_slice_in_dim(rows_c, index_k * BS, BS, 0)
    return (piece_b[:, None, :] * piece_c[None, :, :]).reshape(BS * BS, R).astype(jnp.bfloat16)


def add_block(phi, factor_low, panel, index_i, weight, block_counts):
    block_a = lax.dynamic_slice_in_dim(factor_low, index_i * BS, BS, 0)
    model = lax.dot_general(
        block_a, panel, (((1,), (1,)), ((), ())), preferred_element_type=jnp.float32
    )
    ratio = (block_counts.astype(jnp.float32) / model).astype(jnp.bfloat16)
    part = jnp.dot(ratio, panel, preferred_element_type=jnp.float32) * weight
    old = lax.dynamic_slice_in_dim(phi, index_i * BS, BS, 0)
    return lax.dynamic_update_slice_in_dim(phi, old + part, index_i * BS, 0)


def local(block_coords, live_blocks, counts, factor_a, factor_b, factor_c):
    coords = block_coords.reshape(SLOTS, 3)
    local_counts = counts.reshape(SLOTS, BS, BS * BS)
    weights = (jnp.arange(SLOTS, dtype=jnp.int32) < live_blocks.reshape(())).astype(jnp.float32)
    rows_b = lax.all_gather(factor_b, "ka", axis=0, tiled=True)
    rows_c = lax.all_gather(factor_c, "ia", axis=1, tiled=True)
    sums_b = rows_b.reshape(RB2, BS, R).sum(axis=1)
    sums_c = rows_c.reshape(RB3, BS, R).sum(axis=1)
    pick_j = (coords[:, 1:2] == jnp.arange(RB2, dtype=jnp.int32)[None, :]).astype(jnp.float32)
    pick_k = (coords[:, 2:3] == jnp.arange(RB3, dtype=jnp.int32)[None, :]).astype(jnp.float32)
    masses = jnp.dot(pick_j, sums_b, precision=lax.Precision.HIGHEST) * jnp.dot(
        pick_k, sums_c, precision=lax.Precision.HIGHEST
    )
    pick_i = (coords[:, 0:1] == jnp.arange(RB1, dtype=jnp.int32)[None, :]).astype(
        jnp.float32
    ) * weights[:, None]
    mass_part = lax.dot_general(
        pick_i, masses, (((0,), (0,)), ((), ())), precision=lax.Precision.HIGHEST
    )
    mass = lax.psum(mass_part, ("ja", "ka"))
    mass_rows = jnp.broadcast_to(mass[:, None, :], (RB1, BS, R)).reshape(RB1 * BS, R)
    owned = factor_a.shape[0]
    first_row = lax.axis_index(("ja", "ka")) * owned
    my_mass = lax.dynamic_slice_in_dim(mass_rows, first_row, owned, 0)
    empty = jnp.zeros((RB1 * BS, R), jnp.float32)

    def accumulate(factor_low):

        def step(phi, item):
            index_i, index_j, index_k, weight, block_counts = item
            panel = make_panel(rows_b, rows_c, index_j, index_k)
            return (add_block(phi, factor_low, panel, index_i, weight, block_counts), None)

        phi, _ = lax.scan(
            step, empty, (coords[:, 0], coords[:, 1], coords[:, 2], weights, local_counts)
        )
        return phi

    whole = lax.all_gather(factor_a, ("ja", "ka"), axis=0, tiled=True)
    phi = accumulate(whole.astype(jnp.bfloat16))
    totals = lax.psum(phi, ("ja", "ka"))
    updated = whole * totals / mass_rows
    phi = accumulate(updated.astype(jnp.bfloat16))
    mine = lax.psum_scatter(phi, ("ja", "ka"), scatter_dimension=0, tiled=True)
    return lax.dynamic_slice_in_dim(updated, first_row, owned, 0) * mine / my_mass


def solution(mesh):
    placed = (
        P("ia", "ja", "ka", None, None),
        P("ia", "ja", "ka"),
        P("ia", "ja", "ka", None, None, None),
        P(("ia", "ja", "ka"), None),
        P(("ja", "ka"), None),
        P("ka", "ia"),
    )
    return jax.shard_map(
        local, mesh=mesh, in_specs=placed, out_specs=P(("ia", "ja", "ka"), None), check_vma=False
    )
```

profile of v0, /device:TPU:0, one launch (start us, length us, event | category | flops | bytes accessed | tf_op | source)
XLA Modules:
  0.0 275.6 jit_solution(7233616077265290646)
XLA Ops:
  6.5 0.8 copy.14
  7.5 7.5 %all_gather.11 = f32[256,256]{0,1:T(8,128)S(1)} all-gather(f32[256,64]{0,1:T(8,128)} %param.15), channel_id=1, replica_groups=mesh['ia'=4,'ja'=2,'ka'=4] {'ia'}, dimensions={1}, use_global_device_ids=true | all-gather | bytes 327680 | tf_op jit(solution)/shard_map/all_gather | solution.py:36
  15.1 14.3 %all_gather.10 = f32[256,256]{1,0:T(8,128)S(1)} all-gather(f32[64,256]{1,0:T(8,128)} %param.14), channel_id=1, replica_groups=mesh['ia'=4,'ja'=2,'ka'=4] {'ka'}, dimensions={0}, use_global_device_ids=true | all-gather | bytes 327680 | tf_op jit(solution)/shard_map/all_gather | solution.py:35
  30.1 31.8 %all_gather.9 = f32[256,256]{1,0:T(8,128)S(1)} all-gather(f32[32,256]{1,0:T(8,128)} %param.13), channel_id=1, replica_groups=mesh['ia'=4,'ja'=2,'ka'=4] {'ja','ka'}, dimensions={0}, use_global_device_ids=true | all-gather | bytes 294912 | tf_op jit(solution)/shard_map/all_gather | solution.py:69
  62.0 34.4 %while.20 = (s32[]{:T(128)}, f32[256,256]{1,0:T(8,128)S(1)}, s32[4]{0:T(128)S(1)}, s32[4,64,4096]{2,1,0:T(8,128)}, bf16[256,256]{1,0:T(8,128)(2,1)S(1)}, /*index...) while((s32[]{:T(128)}, f32[256,256]{1,0:T(8,128)S(1)}, ...), condition=%wide.region_1.0_spmd, body=%wide.region_0.0_spmd.sunk | while | flops 271351808 | bytes 7899463 | solution.py:64
  64.7 0.7 multiply_convert_fusion.4
  67.5 3.1 %fusion.52 = f32[256,256]{1,0:T(8,128)S(1)} fusion(f32[256,256]{1,0:T(8,128)S(1)} %get-tuple-element.345, s32[]{:T(128)S(6)} %select_n.33, bf16[4096,256]{1,0:T(8,128)(2,1)S(1)} %bitcast.70, s32[4,64,4096]{2,1,0:T(8,128)} %get-tuple-element.361, s32[]{:T(128)} %get-tuple-element.344, f32[]{:T(128)} %bitcast.60, ...), kind=kOutput, calls=%fused_computation.6.clone.1 | convolution fusion | flops 269254656 | bytes 5408768 | tf_op jit(solution)/shard_map/while/body/eval_jaxpr/dot_general | solution.py:26
  73.3 0.7 multiply_convert_fusion.4
  76.1 3.1 %fusion.52 = f32[256,256]{1,0:T(8,128)S(1)} fusion(f32[256,256]{1,0:T(8,128)S(1)} %get-tuple-element.345, s32[]{:T(128)S(6)} %select_n.33, bf16[4096,256]{1,0:T(8,128)(2,1)S(1)} %bitcast.70, s32[4,64,4096]{2,1,0:T(8,128)} %get-tuple-element.361, s32[]{:T(128)} %get-tuple-element.344, f32[]{:T(128)} %bitcast.60, ...), kind=kOutput, calls=%fused_computation.6.clone.1 | convolution fusion | flops 269254656 | bytes 5408768 | tf_op jit(solution)/shard_map/while/body/eval_jaxpr/dot_general | solution.py:26
  84.7 3.1 %fusion.52 = f32[256,256]{1,0:T(8,128)S(1)} fusion(f32[256,256]{1,0:T(8,128)S(1)} %get-tuple-element.345, s32[]{:T(128)S(6)} %select_n.33, bf16[4096,256]{1,0:T(8,128)(2,1)S(1)} %bitcast.70, s32[4,64,4096]{2,1,0:T(8,128)} %get-tuple-element.361, s32[]{:T(128)} %get-tuple-element.344, f32[]{:T(128)} %bitcast.60, ...), kind=kOutput, calls=%fused_computation.6.clone.1 | convolution fusion | flops 269254656 | bytes 5408768 | tf_op jit(solution)/shard_map/while/body/eval_jaxpr/dot_general | solution.py:26
  90.5 0.7 multiply_convert_fusion.4
  93.3 3.1 %fusion.52 = f32[256,256]{1,0:T(8,128)S(1)} fusion(f32[256,256]{1,0:T(8,128)S(1)} %get-tuple-element.345, s32[]{:T(128)S(6)} %select_n.33, bf16[4096,256]{1,0:T(8,128)(2,1)S(1)} %bitcast.70, s32[4,64,4096]{2,1,0:T(8,128)} %get-tuple-element.361, s32[]{:T(128)} %get-tuple-element.344, f32[]{:T(128)} %bitcast.60, ...), kind=kOutput, calls=%fused_computation.6.clone.1 | convolution fusion | flops 269254656 | bytes 5408768 | tf_op jit(solution)/shard_map/while/body/eval_jaxpr/dot_general | solution.py:26
  96.4 0.7 copy-done.1
  97.9 21.7 %psum.15 = f32[4,256]{1,0:T(4,128)S(1)} all-reduce(f32[4,256]{1,0:T(4,128)S(1)} %fusion.24), channel_id=1, replica_groups=mesh['ia'=4,'ja'=2,'ka'=4] {'ja','ka'}, use_global_device_ids=true, to_apply=%region_5.6 | all-reduce | flops 1024 | bytes 8192 | tf_op jit(solution)/shard_map/psum | solution.py:50
  119.5 49.9 %all-reduce.2.cloned.1.call-done = f32[256,256]{1,0:T(8,128)} async-done(((f32[256,256]{1,0:T(8,128)}), f32[256,256]{1,0:T(8,128)}) %all-reduce.2.cloned.1.call-update) | async-done | bytes 262160 | tf_op jit(solution)/shard_map/psum | solution.py:71
  169.4 1.0 fusion.33
  170.5 34.4 %while.21 = (s32[]{:T(128)}, f32[256,256]{1,0:T(8,128)S(1)}, s32[4]{0:T(128)S(1)}, s32[4,64,4096]{2,1,0:T(8,128)}, bf16[256,256]{1,0:T(8,128)(2,1)S(1)}, /*index...) while((s32[]{:T(128)}, f32[256,256]{1,0:T(8,128)S(1)}, ...), condition=%wide.region_7.8_spmd, body=%wide.region_6.7_spmd.sunk | while | flops 271351808 | bytes 7899463 | solution.py:64
  173.2 0.7 multiply_convert_fusion.5
  176.0 3.1 %fusion.56 = f32[256,256]{1,0:T(8,128)S(1)} fusion(f32[256,256]{1,0:T(8,128)S(1)} %get-tuple-element.387, s32[]{:T(128)S(6)} %select_n.36, bf16[4096,256]{1,0:T(8,128)(2,1)S(1)} %bitcast.71, s32[4,64,4096]{2,1,0:T(8,128)} %get-tuple-element.403, s32[]{:T(128)} %get-tuple-element.386, f32[]{:T(128)} %bitcast.68, ...), kind=kOutput, calls=%fused_computation.20.clone.1 | convolution fusion | flops 269254656 | bytes 5408768 | tf_op jit(solution)/shard_map/while/body/eval_jaxpr/dot_general | solution.py:26
  184.6 3.1 %fusion.56 = f32[256,256]{1,0:T(8,128)S(1)} fusion(f32[256,256]{1,0:T(8,128)S(1)} %get-tuple-element.387, s32[]{:T(128)S(6)} %select_n.36, bf16[4096,256]{1,0:T(8,128)(2,1)S(1)} %bitcast.71, s32[4,64,4096]{2,1,0:T(8,128)} %get-tuple-element.403, s32[]{:T(128)} %get-tuple-element.386, f32[]{:T(128)} %bitcast.68, ...), kind=kOutput, calls=%fused_computation.20.clone.1 | convolution fusion | flops 269254656 | bytes 5408768 | tf_op jit(solution)/shard_map/while/body/eval_jaxpr/dot_general | solution.py:26
  193.2 3.1 %fusion.56 = f32[256,256]{1,0:T(8,128)S(1)} fusion(f32[256,256]{1,0:T(8,128)S(1)} %get-tuple-element.387, s32[]{:T(128)S(6)} %select_n.36, bf16[4096,256]{1,0:T(8,128)(2,1)S(1)} %bitcast.71, s32[4,64,4096]{2,1,0:T(8,128)} %get-tuple-element.403, s32[]{:T(128)} %get-tuple-element.386, f32[]{:T(128)} %bitcast.68, ...), kind=kOutput, calls=%fused_computation.20.clone.1 | convolution fusion | flops 269254656 | bytes 5408768 | tf_op jit(solution)/shard_map/while/body/eval_jaxpr/dot_general | solution.py:26
  201.8 3.1 %fusion.56 = f32[256,256]{1,0:T(8,128)S(1)} fusion(f32[256,256]{1,0:T(8,128)S(1)} %get-tuple-element.387, s32[]{:T(128)S(6)} %select_n.36, bf16[4096,256]{1,0:T(8,128)(2,1)S(1)} %bitcast.71, s32[4,64,4096]{2,1,0:T(8,128)} %get-tuple-element.403, s32[]{:T(128)} %get-tuple-element.386, f32[]{:T(128)} %bitcast.68, ...), kind=kOutput, calls=%fused_computation.20.clone.1 | convolution fusion | flops 269254656 | bytes 5408768 | tf_op jit(solution)/shard_map/while/body/eval_jaxpr/dot_general | solution.py:26
  205.6 61.8 %reduce-scatter.2.cloned.1.call-done = f32[32,256]{1,0:T(8,128)} async-done(((f32[256,256]{1,0:T(8,128)}), f32[32,256]{1,0:T(8,128)}) %reduce-scatter.2.cloned.1.call-update) | async-done | bytes 32784 | tf_op jit(solution)/shard_map/reduce_scatter | solution.py:74
  267.4 1.4 dynamic-slice_divide_fusion
  (63 shorter events, 26.1 us)
Async XLA Ops:
  6.5 162.9 %all-reduce.2.cloned.1.call-start = ((), (), s32[]{:S(2)}) async-start(), calls=%async_computation.1 | async-start | bytes 524288 | tf_op jit(solution)/shard_map/psum | solution.py:71
  96.4 0.7 copy-start.1
  97.1 170.3 %reduce-scatter.2.cloned.1.call-start = ((), (), s32[]{:S(2)}) async-start(), calls=%async_computation.2 | async-start | bytes 294912 | tf_op jit(solution)/shard_map/reduce_scatter | solution.py:74
  204.9 0.7 copy-start
Sparse Core Ops, SparseCore 0:
  97.2 72.1 all-reduce.1
  205.7 61.6 reduce-scatter.1
where the time goes:
time: 277 us; the launch traced here: 276 us
  waiting for transfers between devices  112 us (40%)
  blocking collectives  75.3 us (27%)
  matrix products  25.4 us (9%)
  local copies, waits for them, and re-layouts  24 us (9%)
  loops' own time  17.1 us (6%)
  between operations  14.1 us (5%)
  other arithmetic  7.95 us (3%)
    reduce_scatter x1, waiting for transfers between devices, local(): mine = lax.psum_scatter(phi, ('ja', 'ka'), scatter_dimension=0, tiled=True)  61.8 us
    psum x1, waiting for transfers between devices, local(): totals = lax.psum(phi, ('ja', 'ka'))  49.9 us
    all_gather x1, blocking collectives, local(): whole = lax.all_gather(factor_a, ('ja', 'ka'), axis=0, tiled=True)  31.8 us
    dot_general x8, matrix products, add_block(): part = jnp.dot(ratio, panel, preferred_element_type=jnp.float32) * weight  24.7 us
    psum x1, blocking collectives, local(): mass = lax.psum(mass_part, ('ja', 'ka'))  21.7 us
    dynamic_slice x32, local copies, waits for them, and re-layouts, accumulate(): lax.scan(step, empty, (coords[:, 0], coords[:, 1], coords[:, 2], weights,...  21.4 us
    another operation x2, loops' own time, accumulate(): lax.scan(step, empty, (coords[:, 0], coords[:, 1], coords[:, 2], weights,...  17.1 us
    all_gather x1, blocking collectives, local(): rows_b = lax.all_gather(factor_b, 'ka', axis=0, tiled=True)  14.3 us
  transfers between devices with their start and end apart: 2, of which 2 were waited for; matrix products, arithmetic and copies ran while one was open for 0% of the time, Pallas kernels for 0%

commit v1 on v0

v1 whole, which is shorter than its diff:
```python
import functools

import jax
import jax.numpy as jnp
from jax import lax
from jax.experimental import pallas as pl
from jax.experimental.pallas import tpu as pltpu
from jax.sharding import PartitionSpec as P

RB1 = 4
RB2 = 4
RB3 = 4
MESH = pl.DeviceIdType.MESH


def loop(count, body):
    if count <= 8:
        for d in range(1, count):
            body(d)
    else:

        def step(d, carry):
            body(d)
            return carry

        lax.fori_loop(1, count, step, 0)


def kernel(
    n_ia, n_ja, n_ka, bs,
    coords, live, counts, fa, fb, fc, out,
    cnt, bg, cg, cfull, aown, alow, al, afull, panel, phi, ps, pr, ms, mr,
    local_sem, b_send, b_recv, c_send, c_recv, g_send, g_recv,
):
    n = n_ja * n_ka
    ia, ja, ka = lax.axis_index("ia"), lax.axis_index("ja"), lax.axis_index("ka")
    me = ja * n_ka + ka
    slots = cnt.shape[0]
    owned, rank = aown.shape
    rb = fb.shape[0]
    wc = fc.shape[0]

    def group(d):
        t = lax.rem(me + d, n)
        return {"ja": lax.div(t, n_ka), "ka": lax.rem(t, n_ka)}

    def source(d):
        return lax.rem(me + n - d, n)

    load_a = pltpu.make_async_copy(fa, aown, local_sem.at[0])
    own_rows = pl.ds(pl.multiple_of(ka * rb, rb), rb)
    load_b = pltpu.make_async_copy(fb, bg.at[own_rows], local_sem.at[1])
    own_ranks = pl.ds(pl.multiple_of(ia * wc, wc), wc)
    load_c = pltpu.make_async_copy(fc, cg.at[own_ranks], local_sem.at[2])
    load_n = pltpu.make_async_copy(counts, cnt, local_sem.at[3])
    load_a.start()
    load_b.start()
    load_c.start()
    load_n.start()

    barrier = pltpu.get_barrier_semaphore()
    loop(n, lambda d: pl.semaphore_signal(barrier, inc=1, device_id=group(d), device_id_type=MESH))
    loop(
        n_ia,
        lambda d: pl.semaphore_signal(
            barrier, inc=1, device_id={"ia": lax.rem(ia + d, n_ia)}, device_id_type=MESH
        ),
    )
    load_a.wait()
    alow[0] = aown[...].astype(jnp.bfloat16)
    pl.semaphore_wait(barrier, n + n_ia - 2)

    def b_copy(d, whose):
        rows = pl.ds(pl.multiple_of(whose * rb, rb), rb)
        return pltpu.make_async_remote_copy(
            src_ref=fb, dst_ref=bg.at[rows], send_sem=b_send.at[d], recv_sem=b_recv.at[d],
            device_id={"ka": lax.rem(ka + d, n_ka)}, device_id_type=MESH,
        )

    def c_copy(d, whose):
        ranks = pl.ds(pl.multiple_of(whose * wc, wc), wc)
        return pltpu.make_async_remote_copy(
            src_ref=fc, dst_ref=cg.at[ranks], send_sem=c_send.at[d], recv_sem=c_recv.at[d],
            device_id={"ia": lax.rem(ia + d, n_ia)}, device_id_type=MESH,
        )

    def a_copy(turn, d, whose):
        return pltpu.make_async_remote_copy(
            src_ref=alow.at[turn], dst_ref=al.at[turn, whose],
            send_sem=g_send.at[turn, d], recv_sem=g_recv.at[turn, d],
            device_id=group(d), device_id_type=MESH,
        )

    def phi_copy(turn, d, whose):
        return pltpu.make_async_remote_copy(
            src_ref=ps.at[lax.rem(me + d, n)], dst_ref=pr.at[turn, whose],
            send_sem=g_send.at[2 + turn, d], recv_sem=g_recv.at[2 + turn, d],
            device_id=group(d), device_id_type=MESH,
        )

    def mass_copy(d, whose):
        block = lax.div(lax.rem(me + d, n) * owned, bs)
        return pltpu.make_async_remote_copy(
            src_ref=ms.at[block], dst_ref=mr.at[whose],
            send_sem=g_send.at[4, d], recv_sem=g_recv.at[4, d],
            device_id=group(d), device_id_type=MESH,
        )

    loop(n_ka, lambda d: b_copy(d, ka).start())
    loop(n_ia, lambda d: c_copy(d, ia).start())
    loop(n, lambda d: a_copy(0, d, me).start())

    phi[...] = jnp.zeros_like(phi)
    ms[...] = jnp.zeros_like(ms)
    load_b.wait()
    load_c.wait()
    loop(n_ia, lambda d: c_copy(d, lax.rem(ia + n_ia - d, n_ia)).wait_recv())
    cfull[...] = cg[...].T
    loop(n_ka, lambda d: b_copy(d, lax.rem(ka + n_ka - d, n_ka)).wait_recv())

    def is_block(index, q):
        return jnp.full((bs, rank), index, jnp.int32) == q

    def live_weight(s):
        return jnp.minimum(jnp.maximum(live[0] - s, 0), 1).astype(jnp.float32)

    def piece(ref, index):
        found = ref[:bs]
        for q in range(1, ref.shape[0] // bs):
            found = jnp.where(is_block(index, q), ref[q * bs:(q + 1) * bs], found)
        return found

    def build(s, carry):
        rows_b = piece(bg, coords[s, 1])
        rows_c = piece(cfull, coords[s, 2])
        mass = jnp.sum(rows_b, axis=0, keepdims=True) * jnp.sum(rows_c, axis=0, keepdims=True)
        mass = mass * live_weight(s)
        for q in range(RB1):
            ms[q] += jnp.where(is_block(coords[s, 0], q)[:1], mass, 0.0)
        for j in range(bs):
            panel[s, j * bs:(j + 1) * bs] = (rows_b[j:j + 1] * rows_c).astype(jnp.bfloat16)
        return carry

    lax.fori_loop(0, slots, build, 0)
    loop(n, lambda d: mass_copy(d, me).start())
    mr[me] = ms[lax.div(me * owned, bs)]
    load_n.wait()

    def gathered(turn):
        al[turn, me] = alow[turn]
        loop(n, lambda d: a_copy(turn, d, source(d)).wait_recv())
        for p in range(n):
            afull[p * owned:(p + 1) * owned] = al[turn, p].astype(jnp.float32)

    step_columns = min(1024, bs * bs)

    def accumulate(s, carry):
        block_a = piece(afull, coords[s, 0]).astype(jnp.bfloat16)
        part = jnp.zeros((bs, rank), jnp.float32)
        for first in range(0, bs * bs, step_columns):
            rows = panel[s, first:first + step_columns]
            model = lax.dot_general(
                block_a, rows, (((1,), (1,)), ((), ())), preferred_element_type=jnp.float32
            )
            here = cnt[s, :, first:first + step_columns].astype(jnp.float32)
            ratio = (here / model).astype(jnp.bfloat16)
            part += jnp.dot(ratio, rows, preferred_element_type=jnp.float32)
        part = part * live_weight(s)
        for q in range(RB1):
            phi[q * bs:(q + 1) * bs] += jnp.where(is_block(coords[s, 0], q), part, 0.0)
        return carry

    def scattered(turn):
        for p in range(n):
            ps[p] = phi[p * owned:(p + 1) * owned]
        loop(n, lambda d: phi_copy(turn, d, me).start())
        pr[turn, me] = ps[me]
        loop(n, lambda d: phi_copy(turn, d, source(d)).wait_recv())
        total = pr[turn, 0]
        for p in range(1, n):
            total += pr[turn, p]
        return total

    gathered(0)
    lax.fori_loop(0, slots, accumulate, 0)
    total = scattered(0)
    loop(n, lambda d: mass_copy(d, source(d)).wait_recv())
    mass = mr[0]
    for p in range(1, n):
        mass += mr[p]
    updated = aown[...] * total / mass
    alow[1] = updated.astype(jnp.bfloat16)
    loop(n, lambda d: a_copy(1, d, me).start())
    phi[...] = jnp.zeros_like(phi)
    loop(n, lambda d: phi_copy(0, d, me).wait_send())
    aown[...] = updated
    gathered(1)
    lax.fori_loop(0, slots, accumulate, 0)
    total = scattered(1)
    out[...] = aown[...] * total / mass

    loop(n_ka, lambda d: b_copy(d, ka).wait_send())
    loop(n_ia, lambda d: c_copy(d, ia).wait_send())
    loop(n, lambda d: a_copy(0, d, me).wait_send())
    loop(n, lambda d: a_copy(1, d, me).wait_send())
    loop(n, lambda d: mass_copy(d, me).wait_send())
    loop(n, lambda d: phi_copy(1, d, me).wait_send())


def local(n_ia, n_ja, n_ka, block_coords, live_blocks, counts, factor_a, factor_b, factor_c):
    slots = block_coords.shape[-2]
    bs, cells = counts.shape[-2:]
    owned, rank = factor_a.shape
    rb = factor_b.shape[0]
    rc, wc = factor_c.shape
    n = n_ja * n_ka
    f32, bf16 = jnp.float32, jnp.bfloat16
    smem = pl.BlockSpec(memory_space=pltpu.SMEM)
    hbm = pl.BlockSpec(memory_space=pl.ANY)
    dma = pltpu.SemaphoreType.DMA
    return pl.pallas_call(
        functools.partial(kernel, n_ia, n_ja, n_ka, bs),
        out_shape=jax.ShapeDtypeStruct((owned, rank), f32),
        in_specs=[smem, smem, hbm, hbm, hbm, hbm],
        out_specs=pl.BlockSpec(memory_space=pltpu.VMEM),
        scratch_shapes=[
            pltpu.VMEM((slots, bs, cells), jnp.int32),
            pltpu.VMEM((n_ka * rb, rank), f32),
            pltpu.VMEM((n_ia * wc, rc), f32),
            pltpu.VMEM((rc, rank), f32),
            pltpu.VMEM((owned, rank), f32),
            pltpu.VMEM((2, owned, rank), bf16),
            pltpu.VMEM((2, n, owned, rank), bf16),
            pltpu.VMEM((RB1 * bs, rank), f32),
            pltpu.VMEM((slots, cells, rank), bf16),
            pltpu.VMEM((RB1 * bs, rank), f32),
            pltpu.VMEM((n, owned, rank), f32),
            pltpu.VMEM((2, n, owned, rank), f32),
            pltpu.VMEM((RB1, 1, rank), f32),
            pltpu.VMEM((n, 1, rank), f32),
            dma((4,)),
            dma((n_ka,)),
            dma((n_ka,)),
            dma((n_ia,)),
            dma((n_ia,)),
            dma((5, n)),
            dma((5, n)),
        ],
        compiler_params=pltpu.CompilerParams(
            collective_id=0, has_side_effects=True, vmem_limit_bytes=56 * 1024 * 1024
        ),
    )(
        block_coords.reshape(slots, 3), live_blocks.reshape(1),
        counts.reshape(slots, bs, cells), factor_a, factor_b, factor_c.T,
    )


def solution(mesh):
    placed = (
        P("ia", "ja", "ka", None, None),
        P("ia", "ja", "ka"),
        P("ia", "ja", "ka", None, None, None),
        P(("ia", "ja", "ka"), None),
        P(("ja", "ka"), None),
        P("ka", "ia"),
    )
    body = functools.partial(local, mesh.shape["ia"], mesh.shape["ja"], mesh.shape["ka"])
    return jax.shard_map(
        body, mesh=mesh, in_specs=placed, out_specs=P(("ia", "ja", "ka"), None), check_vma=False
    )
```

time: 277 us -> 48.7 us (0.18)
  waiting for transfers between devices: 112 us -> 0 us
  blocking collectives: 75.3 us -> 0 us
  Pallas kernels: 0 us -> 45.1 us
  matrix products: 25.4 us -> 0 us
  local copies, waits for them, and re-layouts: 24 us -> 2.71 us
  loops' own time: 17.1 us -> 0 us
  between operations: 14.1 us -> 0.66 us
  other arithmetic: 7.95 us -> 0 us
    reduce_scatter x1 -> x0, waiting for transfers between devices: 61.8 us -> none  [local(): mine = lax.psum_scatter(phi, ('ja', 'ka'), scatter_dimension=0, tiled=True)]
    all_gather x3 -> x0, blocking collectives: 53.6 us -> none  [the longest x1 31.8 us: local(): whole = lax.all_gather(factor_a, ('ja', 'ka'), axis=0, tiled=True)]
    psum x1 -> x0, waiting for transfers between devices: 49.9 us -> none  [local(): totals = lax.psum(phi, ('ja', 'ka'))]
    pallas_call x0 -> x1, Pallas kernels: none -> 45.1 us  [local(): pl.pallas_call(functools.partial(kernel, n_ia, n_ja, n_ka, bs), out_shape...]
    dot_general x11 -> x0, matrix products: 25.4 us -> none  [the longest x8 24.7 us: add_block(): part = jnp.dot(ratio, panel, preferred_element_type=jnp.float32) * weight]
    psum x1 -> x0, blocking collectives: 21.7 us -> none  [local(): mass = lax.psum(mass_part, ('ja', 'ka'))]
    dynamic_slice x40 -> x0, local copies, waits for them, and re-layouts: 21.5 us -> none  [the longest x32 21.4 us: accumulate(): lax.scan(step, empty, (coords[:, 0], coords[:, 1], coords[:, 2], weights,...]
    another operation x2 -> x0, loops' own time: 17.1 us -> none  [accumulate(): lax.scan(step, empty, (coords[:, 0], coords[:, 1], coords[:, 2], weights,...]
  transfers between devices with their start and end apart: 2 -> 0, of which waited for: 2 -> 0; matrix products, arithmetic and copies ran while one was open for 0% -> 0% of each run, Pallas kernels for 0% -> 0%
where the time goes in v1:
time: 48.7 us; the launch traced here: 48.4 us
  Pallas kernels  45.1 us (93%)
  local copies, waits for them, and re-layouts  2.71 us (6%)
  between operations  0.66 us (1%)
    pallas_call x1, Pallas kernels, local(): pl.pallas_call(functools.partial(kernel, n_ia, n_ja, n_ka, bs), out_shape...  45.1 us
    unnamed x2, local copies, waits for them, and re-layouts  2.71 us

profile of v1, /device:TPU:0, one launch (start us, length us, event | category | flops | bytes accessed | tf_op | source)
XLA Modules:
  0.0 48.4 jit_solution(8963399225356388188)
XLA Ops:
  0.7 1.3 %copy.7 = s32[1,1,1,4,3]{4,3,2,1,0:T(4,128)} copy(s32[1,1,1,4,3]{3,2,4,1,0:T(1,128)} %param.6) | data formatting | bytes 96 | tf_op args[0]
  2.0 45.1 %shard_map.64 = f32[32,256]{1,0:T(8,128)} custom-call(s32[4,3]{1,0:T(4,128)} %bitcast.7, s32[1]{0:T(128)} %bitcast.4.live, s32[4,64,4096]{2,1,0:T(8,128)} %bitcast.5, f32[32,256]{1,0:T(8,128)} %fa.1, f32[64,256]{1,0:T(8,128)} %fb.1, f32[64,256]{1,0:T(8,128)} %bitcast.6), custom_call_target="tpu_custom_call" | custom-call | tf_op jit(solution)/shard_map/pallas_call | solution.py:221
  47.1 1.4 %copy.10 = f32[32,256]{1,0:T(8,128)} copy(f32[32,256]{1,0:T(8,128)} %shard_map.64) | data formatting | bytes 65536

commit v2 on v1

--- a/solution.py
+++ b/solution.py
@@ -59,22 +59,37 @@
     load_n.start()
 
     barrier = pltpu.get_barrier_semaphore()
-    loop(n, lambda d: pl.semaphore_signal(barrier, inc=1, device_id=group(d), device_id_type=MESH))
-    loop(
-        n_ia,
-        lambda d: pl.semaphore_signal(
-            barrier, inc=1, device_id={"ia": lax.rem(ia + d, n_ia)}, device_id_type=MESH
-        ),
-    )
+    for axis, here, count in (("ka", ka, n_ka), ("ja", ja, n_ja), ("ia", ia, n_ia)):
+        loop(
+            count,
+            lambda d: pl.semaphore_signal(
+                barrier, inc=1, device_id={axis: lax.rem(here + d, count)}, device_id_type=MESH
+            ),
+        )
     load_a.wait()
     alow[0] = aown[...].astype(jnp.bfloat16)
-    pl.semaphore_wait(barrier, n + n_ia - 2)
+    pl.semaphore_wait(barrier, n_ka + n_ja + n_ia - 3)
+
+    halves = 2 if n_ia % 2 == 0 and rb % 16 == 0 else 1
+    hb = rb // halves
+    part = lax.rem(ia, halves)
+    partner = ia + 1 - 2 * part
+
+    def b_rows(whose, half):
+        return bg.at[pl.ds(pl.multiple_of(whose * rb + half * hb, hb), hb)]
 
     def b_copy(d, whose):
-        rows = pl.ds(pl.multiple_of(whose * rb, rb), rb)
-        return pltpu.make_async_remote_copy(
-            src_ref=fb, dst_ref=bg.at[rows], send_sem=b_send.at[d], recv_sem=b_recv.at[d],
+        return pltpu.make_async_remote_copy(
+            src_ref=fb.at[pl.ds(pl.multiple_of(part * hb, hb), hb)], dst_ref=b_rows(whose, part),
+            send_sem=b_send.at[0, d], recv_sem=b_recv.at[0, d],
             device_id={"ka": lax.rem(ka + d, n_ka)}, device_id_type=MESH,
+        )
+
+    def b_hand(d, half):
+        rows = b_rows(lax.rem(ka + n_ka - d, n_ka), half)
+        return pltpu.make_async_remote_copy(
+            src_ref=rows, dst_ref=rows, send_sem=b_send.at[1, d], recv_sem=b_recv.at[1, d],
+            device_id={"ia": partner}, device_id_type=MESH,
         )
 
     def c_copy(d, whose):
@@ -84,11 +99,27 @@
             device_id={"ia": lax.rem(ia + d, n_ia)}, device_id_type=MESH,
         )
 
-    def a_copy(turn, d, whose):
-        return pltpu.make_async_remote_copy(
-            src_ref=alow.at[turn], dst_ref=al.at[turn, whose],
-            send_sem=g_send.at[turn, d], recv_sem=g_recv.at[turn, d],
+    def a_copy(d, whose):
+        return pltpu.make_async_remote_copy(
+            src_ref=alow.at[1], dst_ref=al.at[1, whose],
+            send_sem=g_send.at[1, d], recv_sem=g_recv.at[1, d],
             device_id=group(d), device_id_type=MESH,
+        )
+
+    def a_across(d, whose):
+        return pltpu.make_async_remote_copy(
+            src_ref=alow.at[0], dst_ref=al.at[0, whose * n_ka + ka],
+            send_sem=g_send.at[0, d * n_ka], recv_sem=g_recv.at[0, d * n_ka],
+            device_id={"ja": lax.rem(ja + d, n_ja)}, device_id_type=MESH,
+        )
+
+    def a_along(e, d, whose):
+        other = lax.rem(ja + n_ja - e, n_ja) * n_ka
+        return pltpu.make_async_remote_copy(
+            src_ref=alow.at[0] if isinstance(e, int) and e == 0 else al.at[0, other + ka],
+            dst_ref=al.at[0, other + whose],
+            send_sem=g_send.at[0, e * n_ka + d], recv_sem=g_recv.at[0, e * n_ka + d],
+            device_id={"ka": lax.rem(ka + d, n_ka)}, device_id_type=MESH,
         )
 
     def phi_copy(turn, d, whose):
@@ -108,15 +139,32 @@
 
     loop(n_ka, lambda d: b_copy(d, ka).start())
     loop(n_ia, lambda d: c_copy(d, ia).start())
-    loop(n, lambda d: a_copy(0, d, me).start())
+    loop(n_ja, lambda d: a_across(d, ja).start())
+    loop(n_ka, lambda d: a_along(0, d, ka).start())
+    al[0, me] = alow[0]
 
     phi[...] = jnp.zeros_like(phi)
     ms[...] = jnp.zeros_like(ms)
     load_b.wait()
     load_c.wait()
+
+
+    def across(e):
+        a_across(e, lax.rem(ja + n_ja - e, n_ja)).wait_recv()
+        loop(n_ka, lambda d: a_along(e, d, ka).start())
+
+    loop(n_ja, across)
+
+    def hand_on(d):
+        b_copy(d, lax.rem(ka + n_ka - d, n_ka)).wait_recv()
+        if halves == 2:
+            b_hand(d, part).start()
+
+    loop(n_ka, hand_on)
     loop(n_ia, lambda d: c_copy(d, lax.rem(ia + n_ia - d, n_ia)).wait_recv())
     cfull[...] = cg[...].T
-    loop(n_ka, lambda d: b_copy(d, lax.rem(ka + n_ka - d, n_ka)).wait_recv())
+    if halves == 2:
+        loop(n_ka, lambda d: b_hand(d, 1 - part).wait_recv())
 
     def is_block(index, q):
         return jnp.full((bs, rank), index, jnp.int32) == q
@@ -131,34 +179,40 @@
         return found
 
     def build(s, carry):
-        rows_b = piece(bg, coords[s, 1])
-        rows_c = piece(cfull, coords[s, 2])
+        rows_b = piece(bg, coords[1, 0, s])
+        rows_c = piece(cfull, coords[2, 0, s])
         mass = jnp.sum(rows_b, axis=0, keepdims=True) * jnp.sum(rows_c, axis=0, keepdims=True)
         mass = mass * live_weight(s)
         for q in range(RB1):
-            ms[q] += jnp.where(is_block(coords[s, 0], q)[:1], mass, 0.0)
-        for j in range(bs):
-            panel[s, j * bs:(j + 1) * bs] = (rows_b[j:j + 1] * rows_c).astype(jnp.bfloat16)
+            ms[q] += jnp.where(is_block(coords[0, 0, s], q)[:1], mass, 0.0)
         return carry
 
     lax.fori_loop(0, slots, build, 0)
-    loop(n, lambda d: mass_copy(d, me).start())
     mr[me] = ms[lax.div(me * owned, bs)]
     load_n.wait()
 
-    def gathered(turn):
-        al[turn, me] = alow[turn]
-        loop(n, lambda d: a_copy(turn, d, source(d)).wait_recv())
+    def spread(turn):
         for p in range(n):
             afull[p * owned:(p + 1) * owned] = al[turn, p].astype(jnp.float32)
 
     step_columns = min(1024, bs * bs)
 
-    def accumulate(s, carry):
-        block_a = piece(afull, coords[s, 0]).astype(jnp.bfloat16)
+    def accumulate(s, carry, fresh=False):
+        if fresh:
+            rows_b, rows_c = piece(bg, coords[1, 0, s]), piece(cfull, coords[2, 0, s])
+        block_a = piece(afull, coords[0, 0, s]).astype(jnp.bfloat16)
         part = jnp.zeros((bs, rank), jnp.float32)
         for first in range(0, bs * bs, step_columns):
-            rows = panel[s, first:first + step_columns]
+            if fresh:
+                rows = jnp.concatenate(
+                    [
+                        (rows_b[j:j + 1] * rows_c).astype(jnp.bfloat16)
+                        for j in range(first // bs, (first + step_columns) // bs)
+                    ]
+                )
+                panel[s, first:first + step_columns] = rows
+            else:
+                rows = panel[s, first:first + step_columns]
             model = lax.dot_general(
                 block_a, rows, (((1,), (1,)), ((), ())), preferred_element_type=jnp.float32
             )
@@ -167,7 +221,7 @@
             part += jnp.dot(ratio, rows, preferred_element_type=jnp.float32)
         part = part * live_weight(s)
         for q in range(RB1):
-            phi[q * bs:(q + 1) * bs] += jnp.where(is_block(coords[s, 0], q), part, 0.0)
+            phi[q * bs:(q + 1) * bs] += jnp.where(is_block(coords[0, 0, s], q), part, 0.0)
         return carry
 
     def scattered(turn):
@@ -181,8 +235,11 @@
             total += pr[turn, p]
         return total
 
-    gathered(0)
-    lax.fori_loop(0, slots, accumulate, 0)
+    for e in range(n_ja):
+        loop(n_ka, lambda d: a_along(e, d, lax.rem(ka + n_ka - d, n_ka)).wait_recv())
+    spread(0)
+    loop(n, lambda d: mass_copy(d, me).start())
+    lax.fori_loop(0, slots, functools.partial(accumulate, fresh=True), 0, unroll=True)
     total = scattered(0)
     loop(n, lambda d: mass_copy(d, source(d)).wait_recv())
     mass = mr[0]
@@ -190,19 +247,25 @@
         mass += mr[p]
     updated = aown[...] * total / mass
     alow[1] = updated.astype(jnp.bfloat16)
-    loop(n, lambda d: a_copy(1, d, me).start())
+    loop(n, lambda d: a_copy(d, me).start())
     phi[...] = jnp.zeros_like(phi)
     loop(n, lambda d: phi_copy(0, d, me).wait_send())
     aown[...] = updated
-    gathered(1)
-    lax.fori_loop(0, slots, accumulate, 0)
+    al[1, me] = alow[1]
+    loop(n, lambda d: a_copy(d, source(d)).wait_recv())
+    spread(1)
+    lax.fori_loop(0, slots, accumulate, 0, unroll=True)
     total = scattered(1)
     out[...] = aown[...] * total / mass
 
     loop(n_ka, lambda d: b_copy(d, ka).wait_send())
     loop(n_ia, lambda d: c_copy(d, ia).wait_send())
-    loop(n, lambda d: a_copy(0, d, me).wait_send())
-    loop(n, lambda d: a_copy(1, d, me).wait_send())
+    if halves == 2:
+        loop(n_ka, lambda d: b_hand(d, part).wait_send())
+    loop(n_ja, lambda d: a_across(d, ja).wait_send())
+    for e in range(n_ja):
+        loop(n_ka, lambda d: a_along(e, d, ka).wait_send())
+    loop(n, lambda d: a_copy(d, me).wait_send())
     loop(n, lambda d: mass_copy(d, me).wait_send())
     loop(n, lambda d: phi_copy(1, d, me).wait_send())
 
@@ -239,8 +302,8 @@
             pltpu.VMEM((RB1, 1, rank), f32),
             pltpu.VMEM((n, 1, rank), f32),
             dma((4,)),
-            dma((n_ka,)),
-            dma((n_ka,)),
+            dma((2, n_ka)),
+            dma((2, n_ka)),
             dma((n_ia,)),
             dma((n_ia,)),
             dma((5, n)),
@@ -250,7 +313,7 @@
             collective_id=0, has_side_effects=True, vmem_limit_bytes=56 * 1024 * 1024
         ),
     )(
-        block_coords.reshape(slots, 3), live_blocks.reshape(1),
+        jnp.swapaxes(block_coords, 3, 4).reshape(3, 1, slots), live_blocks.reshape(1),
         counts.reshape(slots, bs, cells), factor_a, factor_b, factor_c.T,
     )
 

time: 48.7 us -> 44.2 us (0.908)
  Pallas kernels: 45.1 us -> 42 us
  local copies, waits for them, and re-layouts: 2.71 us -> 1.38 us
    pallas_call x1, Pallas kernels: 45.1 us -> 42 us  [local(): pl.pallas_call(functools.partial(kernel, n_ia, n_ja, n_ka, bs), out_shape...]
    unnamed x2 -> x1, local copies, waits for them, and re-layouts: 2.71 us -> 1.38 us
where the time goes in v2:
time: 44.2 us; the launch traced here: 44 us
  Pallas kernels  42 us (95%)
  local copies, waits for them, and re-layouts  1.38 us (3%)
  between operations  0.66 us (1%)
    pallas_call x1, Pallas kernels, local(): pl.pallas_call(functools.partial(kernel, n_ia, n_ja, n_ka, bs), out_shape...  42 us
    unnamed x1, local copies, waits for them, and re-layouts  1.38 us

profile of v2, /device:TPU:0, one launch (start us, length us, event | category | flops | bytes accessed | tf_op | source)
XLA Modules:
  0.0 44.0 jit_solution(5318827950830515079)
XLA Ops:
  0.7 42.0 %shard_map.64 = f32[32,256]{1,0:T(8,128)} custom-call(s32[3,1,4]{2,1,0:T(1,128)} %bitcast.9, s32[1]{0:T(128)} %bitcast.6.live, s32[4,64,4096]{2,1,0:T(8,128)} %bitcast.7, f32[32,256]{1,0:T(8,128)} %fa.1, f32[64,256]{1,0:T(8,128)} %fb.1, f32[64,256]{1,0:T(8,128)} %bitcast.8), custom_call_target="tpu_custom_call" | custom-call | tf_op jit(solution)/shard_map/pallas_call | solution.py:284
  42.7 1.4 %copy.9 = f32[32,256]{1,0:T(8,128)} copy(f32[32,256]{1,0:T(8,128)} %shard_map.64) | data formatting | bytes 65536

commit v3 on v2

--- a/solution.py
+++ b/solution.py
@@ -13,9 +13,9 @@
 MESH = pl.DeviceIdType.MESH
 
 
-def loop(count, body):
+def loop(count, body, order=None):
     if count <= 8:
-        for d in range(1, count):
+        for d in order or range(1, count):
             body(d)
     else:
 
@@ -28,7 +28,7 @@
 
 def kernel(
     n_ia, n_ja, n_ka, bs,
-    coords, live, counts, fa, fb, fc, out,
+    coords_in, live_in, counts, fa, fb, fc, out, coords, live,
     cnt, bg, cg, cfull, aown, alow, al, afull, panel, phi, ps, pr, ms, mr,
     local_sem, b_send, b_recv, c_send, c_recv, g_send, g_recv,
 ):
@@ -40,6 +40,8 @@
     rb = fb.shape[0]
     wc = fc.shape[0]
 
+    far_first = sorted(range(1, n), key=lambda d: -min(d % n_ka, n_ka - d % n_ka))
+
     def group(d):
         t = lax.rem(me + d, n)
         return {"ja": lax.div(t, n_ka), "ka": lax.rem(t, n_ka)}
@@ -57,6 +59,10 @@
     load_b.start()
     load_c.start()
     load_n.start()
+    load_where = pltpu.make_async_copy(coords_in, coords, local_sem.at[4])
+    load_live = pltpu.make_async_copy(live_in, live, local_sem.at[5])
+    load_where.start()
+    load_live.start()
 
     barrier = pltpu.get_barrier_semaphore()
     for axis, here, count in (("ka", ka, n_ka), ("ja", ja, n_ja), ("ia", ia, n_ia)):
@@ -145,6 +151,8 @@
 
     phi[...] = jnp.zeros_like(phi)
     ms[...] = jnp.zeros_like(ms)
+    load_where.wait()
+    load_live.wait()
     load_b.wait()
     load_c.wait()
 
@@ -197,12 +205,11 @@
 
     step_columns = min(1024, bs * bs)
 
-    def accumulate(s, carry, fresh=False):
-        if fresh:
-            rows_b, rows_c = piece(bg, coords[1, 0, s]), piece(cfull, coords[2, 0, s])
-        block_a = piece(afull, coords[0, 0, s]).astype(jnp.bfloat16)
-        part = jnp.zeros((bs, rank), jnp.float32)
-        for first in range(0, bs * bs, step_columns):
+    steps = [(s, first) for s in range(slots) for first in range(0, bs * bs, step_columns)]
+
+    def accumulate(fresh):
+        def model_of(item, block_a, rows_b, rows_c):
+            s, first = item
             if fresh:
                 rows = jnp.concatenate(
                     [
@@ -216,18 +223,37 @@
             model = lax.dot_general(
                 block_a, rows, (((1,), (1,)), ((), ())), preferred_element_type=jnp.float32
             )
+            return rows, model
+
+        def start(item):
+            s, first = item
+            if first == 0:
+                block_a = piece(afull, coords[0, 0, s]).astype(jnp.bfloat16)
+                held[:] = [block_a, None, None]
+                if fresh:
+                    held[1:] = [piece(bg, coords[1, 0, s]), piece(cfull, coords[2, 0, s])]
+            return model_of(item, *held)
+
+        held = []
+        part = None
+        ahead = start(steps[0])
+        for at, (s, first) in enumerate(steps):
+            rows, model = ahead
+            if at + 1 < len(steps):
+                ahead = start(steps[at + 1])
             here = cnt[s, :, first:first + step_columns].astype(jnp.float32)
             ratio = (here / model).astype(jnp.bfloat16)
-            part += jnp.dot(ratio, rows, preferred_element_type=jnp.float32)
-        part = part * live_weight(s)
-        for q in range(RB1):
-            phi[q * bs:(q + 1) * bs] += jnp.where(is_block(coords[0, 0, s], q), part, 0.0)
-        return carry
+            term = jnp.dot(ratio, rows, preferred_element_type=jnp.float32)
+            part = term if first == 0 else part + term
+            if first + step_columns == bs * bs:
+                part = part * live_weight(s)
+                for q in range(RB1):
+                    phi[q * bs:(q + 1) * bs] += jnp.where(is_block(coords[0, 0, s], q), part, 0.0)
 
     def scattered(turn):
         for p in range(n):
             ps[p] = phi[p * owned:(p + 1) * owned]
-        loop(n, lambda d: phi_copy(turn, d, me).start())
+        loop(n, lambda d: phi_copy(turn, d, me).start(), far_first)
         pr[turn, me] = ps[me]
         loop(n, lambda d: phi_copy(turn, d, source(d)).wait_recv())
         total = pr[turn, 0]
@@ -239,7 +265,7 @@
         loop(n_ka, lambda d: a_along(e, d, lax.rem(ka + n_ka - d, n_ka)).wait_recv())
     spread(0)
     loop(n, lambda d: mass_copy(d, me).start())
-    lax.fori_loop(0, slots, functools.partial(accumulate, fresh=True), 0, unroll=True)
+    accumulate(True)
     total = scattered(0)
     loop(n, lambda d: mass_copy(d, source(d)).wait_recv())
     mass = mr[0]
@@ -247,14 +273,14 @@
         mass += mr[p]
     updated = aown[...] * total / mass
     alow[1] = updated.astype(jnp.bfloat16)
-    loop(n, lambda d: a_copy(d, me).start())
+    loop(n, lambda d: a_copy(d, me).start(), far_first)
     phi[...] = jnp.zeros_like(phi)
     loop(n, lambda d: phi_copy(0, d, me).wait_send())
     aown[...] = updated
     al[1, me] = alow[1]
     loop(n, lambda d: a_copy(d, source(d)).wait_recv())
     spread(1)
-    lax.fori_loop(0, slots, accumulate, 0, unroll=True)
+    accumulate(False)
     total = scattered(1)
     out[...] = aown[...] * total / mass
 
@@ -278,15 +304,16 @@
     rc, wc = factor_c.shape
     n = n_ja * n_ka
     f32, bf16 = jnp.float32, jnp.bfloat16
-    smem = pl.BlockSpec(memory_space=pltpu.SMEM)
     hbm = pl.BlockSpec(memory_space=pl.ANY)
     dma = pltpu.SemaphoreType.DMA
     return pl.pallas_call(
         functools.partial(kernel, n_ia, n_ja, n_ka, bs),
         out_shape=jax.ShapeDtypeStruct((owned, rank), f32),
-        in_specs=[smem, smem, hbm, hbm, hbm, hbm],
+        in_specs=[hbm] * 6,
         out_specs=pl.BlockSpec(memory_space=pltpu.VMEM),
         scratch_shapes=[
+            pltpu.SMEM((3, 1, slots), jnp.int32),
+            pltpu.SMEM((1,), jnp.int32),
             pltpu.VMEM((slots, bs, cells), jnp.int32),
             pltpu.VMEM((n_ka * rb, rank), f32),
             pltpu.VMEM((n_ia * wc, rc), f32),
@@ -301,7 +328,7 @@
             pltpu.VMEM((2, n, owned, rank), f32),
             pltpu.VMEM((RB1, 1, rank), f32),
             pltpu.VMEM((n, 1, rank), f32),
-            dma((4,)),
+            dma((6,)),
             dma((2, n_ka)),
             dma((2, n_ka)),
             dma((n_ia,)),

time: 44.2 us -> 42.2 us (0.955)
  Pallas kernels: 42 us -> 40 us
    pallas_call x1, Pallas kernels: 42 us -> 40 us  [local(): pl.pallas_call(functools.partial(kernel, n_ia, n_ja, n_ka, bs), out_shape...]
where the time goes in v3:
time: 42.2 us; the launch traced here: 42 us
  Pallas kernels  40 us (95%)
  local copies, waits for them, and re-layouts  1.38 us (3%)
  between operations  0.66 us (2%)
    pallas_call x1, Pallas kernels, local(): pl.pallas_call(functools.partial(kernel, n_ia, n_ja, n_ka, bs), out_shape...  40 us
    unnamed x1, local copies, waits for them, and re-layouts  1.38 us

profile of v3, /device:TPU:0, one launch (start us, length us, event | category | flops | bytes accessed | tf_op | source)
XLA Modules:
  0.0 42.0 jit_solution(13302472817862285661)
XLA Ops:
  0.7 40.0 %shard_map.64 = f32[32,256]{1,0:T(8,128)} custom-call(s32[3,1,4]{2,1,0:T(1,128)} %bitcast.9, s32[1]{0:T(128)} %bitcast.6.live_in, s32[4,64,4096]{2,1,0:T(8,128)} %bitcast.7, f32[32,256]{1,0:T(8,128)} %fa.1, f32[64,256]{1,0:T(8,128)} %fb.1, f32[64,256]{1,0:T(8,128)} %bitcast.8), custom_call_target="tpu_custom_call" | custom-call | tf_op jit(solution)/shard_map/pallas_call | solution.py:309
  40.7 1.4 %copy.9 = f32[32,256]{1,0:T(8,128)} copy(f32[32,256]{1,0:T(8,128)} %shard_map.64) | data formatting | bytes 65536
